TPU v7x, 512 devices: a whole 4x4x16 slice. The times are simulated.
512 devices in a mesh: seq: 64 (over z_lo, y, core), chan: 8 (over z_hi, x).
Axes of the slice: x: 4, y: 4, z: 16 (z_hi: 2, z_lo: 8; z = z_hi * 8 + z_lo), core: 2. Of those that a mesh axis runs over, the one named last changes fastest.
Arguments:
- inputs: bfloat16 [8192, 8192], P('seq', 'chan'), may hold values from -256 to 256
- gating: bfloat16 [8192, 8192], P('seq', 'chan'), may hold values from -6 to 6
- long_filter: bfloat16 [513, 8192], P(None, 'chan'), may hold values from -0.25 to 0.25
- skip_scale: float32 [8192], P('chan'), may hold values from 0.5 to 1.5
Outputs:
- gated: bfloat16 [8192, 8192], P('seq', 'chan')
All inputs are finite; a program needn't handle non-finite values.
Results may differ from a plain program's by a relative error of at most 0.0049.
Values may be sent and summed in bfloat16 or wider, within the bound.
A program may use at most 64 MiB of HBM per device.

v0:
```python
import math

import jax
import jax.numpy as jnp
from jax import lax
from jax.sharding import PartitionSpec as P

D = 8192
LAGS = 4


def passed_along(value, axis, steps):
    count = lax.axis_size(axis)
    leading, last = (max(0, -steps), min(count, count - steps))
    return lax.ppermute(value, axis, [(source, source + steps) for source in range(leading, last)])


def product_hi(left, right):
    return jnp.dot(left, right, precision=lax.Precision.HIGHEST, preferred_element_type=jnp.float32)


def multiply(left, right):
    return (left[0] * right[0] - left[1] * right[1], left[0] * right[1] + left[1] * right[0])


def on_device(inputs, gating, long_filter, skip_scale):
    tok_rows, channels = inputs.shape
    values = inputs.astype(jnp.float32)
    square_sum = lax.psum(jnp.sum(values * values, axis=1), "chan")
    normed = (values * lax.rsqrt(square_sum[:, None] / D + 1e-06)).astype(jnp.bfloat16)
    points = 2 * tok_rows
    index_row = lax.optimization_barrier(jnp.arange(points, dtype=jnp.int32))
    phase_index = index_row[:, None] * index_row[None, :] % points
    angles = phase_index.astype(jnp.float32) * (2.0 * math.pi / points)
    cosine_table = jnp.cos(angles)
    sine_table = jnp.sin(angles)
    padded = jnp.concatenate(
        [
            jnp.zeros((tok_rows, channels), jnp.bfloat16),
            long_filter,
            jnp.zeros((tok_rows - 1, channels), jnp.bfloat16),
        ],
        0,
    )
    keep_rows = (jnp.arange(tok_rows) > 0).astype(jnp.float32)[:, None]

    def shaped_segment(lag_start):
        segment = lax.dynamic_slice_in_dim(padded, lag_start, points, 0).astype(jnp.float32)
        return jnp.concatenate([segment[tok_rows:], segment[:tok_rows] * keep_rows], 0)

    stacked = jnp.concatenate([shaped_segment(offset * tok_rows) for offset in range(LAGS + 1)], 1)
    all_real = product_hi(cosine_table, stacked)
    all_imag = -product_hi(sine_table, stacked)
    spectra = [
        (
            all_real[:, offset * channels : (offset + 1) * channels],
            all_imag[:, offset * channels : (offset + 1) * channels],
        )
        for offset in range(LAGS + 1)
    ]
    travelling = normed
    acc_real = jnp.zeros((points, channels), jnp.float32)
    acc_imag = jnp.zeros((points, channels), jnp.float32)
    for offset in range(LAGS + 1):
        if offset > 0:
            source = travelling
            stride = 1
            travelling = passed_along(source, "seq", stride)
        signal = travelling.astype(jnp.float32)
        product = multiply(
            (
                product_hi(cosine_table[:, :tok_rows], signal),
                -product_hi(sine_table[:, :tok_rows], signal),
            ),
            spectra[offset],
        )
        acc_real = acc_real + product[0]
        acc_imag = acc_imag + product[1]
    convolved = (
        product_hi(cosine_table[:tok_rows], acc_real) - product_hi(sine_table[:tok_rows], acc_imag)
    ) / points
    mixed = gating.astype(jnp.float32) * (
        convolved + skip_scale[None, :] * normed.astype(jnp.float32)
    )
    return mixed.astype(jnp.bfloat16)


def solution(mesh):
    in_specs = (P("seq", "chan"), P("seq", "chan"), P(None, "chan"), P("chan"))
    out_specs = P("seq", "chan")
    return jax.shard_map(
        on_device, mesh=mesh, in_specs=in_specs, out_specs=out_specs, check_vma=False
    )
```

profile of v0, /device:TPU:32, one launch (start us, length us, event | category | flops | bytes accessed | tf_op | source)
XLA Modules:
  0.0 106.7 jit_solution(4354993777656333287)
XLA Ops:
  0.0 1.1 %fusion.63 = f32[128]{0:T(128)S(1)} fusion(bf16[128,1024]{1,0:T(8,128)(2,1)} %param.4), kind=kLoop, calls=%fused_computation.79 | loop fusion | flops 393088 | bytes 262656 | tf_op jit(solution)/shard_map/reduce_sum | solution.py:29
  1.1 48.5 %psum.7 = f32[128]{0:T(128)S(1)} all-reduce(f32[128]{0:T(128)S(1)} %fusion.63), channel_id=1, replica_groups=mesh['seq'=64,'chan'=8] {'chan'}, use_global_device_ids=true, to_apply=%region_1.0 | all-reduce | flops 128 | bytes 1024 | tf_op jit(solution)/shard_map/psum | solution.py:29
  49.6 1.1 fusion.64
  50.6 1.9 %collective-permute-start = (bf16[128,1024]{1,0:T(8,128)(2,1)S(1)}, bf16[128,1024]{1,0:T(8,128)(2,1)S(1)}, u32[]{:S(2)}, u32[]{:S(2)}) collective-permute-start(bf16[128,1024]{1,0:T(8,128)(2,1)S(1)} %fusion.64), channel_id=1, source_target_pairs={{0,8},{8,16},{16,24},{24,32},{32,40},{40,48},{48,56},{56,64},{64,7... | collective-permute-start | bytes 786440 | tf_op jit(solution)/shard_map/ppermute | solution.py:15
  52.6 2.1 %fusion.65 = (f32[256,1024]{1,0:T(8,128)S(1)}, f32[256,1024]{1,0:T(8,128)S(1)}, f32[256,1024]{1,0:T(8,128)S(1)}, f32[256,1024]{1,0:T(8,128)S(1)}, f32[256,1024]{1,0:T(8,128)S(1)}) fusion(bf16[513,1024]{1,0:T(8,128)(2,1)} %param.6), kind=kLoop, calls=%fused_computation.81 | loop fusion | flops 1310720 | bytes 7880704 | tf_op jit(solution)/shard_map/convert_element_type | solution.py:48
  54.7 0.1 fusion.104
  54.9 0.2 fusion.102
  55.1 0.2 fusion.100
  55.3 0.1 maximum_dynamic-update-slice_fusion.3
  55.4 0.1 maximum_dynamic-update-slice_fusion.2
  55.5 0.1 maximum_dynamic-update-slice_fusion.1
  55.7 6.1 %fusion.89 = f32[256,5120]{1,0:T(8,128)S(1)} fusion(f32[256,5120]{1,0:T(8,128)S(1)} %maximum_dynamic-update-slice_fusion, s32[256]{0:T(256)S(1)} %iota.16), kind=kOutput, calls=%fused_computation.118 | convolution fusion | flops 4027449344 | bytes 10486784 | tf_op jit(solution)/shard_map/dot_general | solution.py:19
  61.9 6.4 %convolution_negate_fusion = f32[256,5120]{1,0:T(8,128)S(1)} fusion(f32[256,5120]{1,0:T(8,128)S(1)} %maximum_dynamic-update-slice_fusion, s32[256]{0:T(256)S(1)} %iota.16), kind=kOutput, calls=%fused_computation | convolution fusion | flops 4028760064 | bytes 10486784 | tf_op jit(solution)/shard_map/dot_general | solution.py:19
  68.2 1.1 %fusion.73 = (f32[256,256]{1,0:T(8,128)S(1)}, f32[256,256]{1,0:T(8,128)S(1)}) fusion(s32[256]{0:T(256)S(1)} %iota.16), kind=kLoop, calls=%fused_computation.102 | loop fusion | flops 917504 | bytes 525312 | tf_op jit(solution)/shard_map/cos | solution.py:35
  69.3 0.6 convolution_negate_fusion.5
  69.9 0.6 fusion.87
  70.5 3.6 %collective-permute-start.1 = (bf16[128,1024]{1,0:T(8,128)(2,1)S(1)}, bf16[128,1024]{1,0:T(8,128)(2,1)S(1)}, u32[]{:S(2)}, u32[]{:S(2)}) collective-permute-start(bf16[128,1024]{1,0:T(8,128)(2,1)S(1)} %collective-permute-done), channel_id=1, source_target_pairs={{0,8},{8,16},{16,24},{24,32},{32,40},{40,48},{48,56},{56,64},{64,7... | collective-permute-start | bytes 786440 | tf_op jit(solution)/shard_map/ppermute | solution.py:15
  74.1 0.6 convolution_negate_fusion.4
  74.7 0.6 fusion.85
  75.2 5.1 %collective-permute-done.1 = bf16[128,1024]{1,0:T(8,128)(2,1)S(1)} collective-permute-done((bf16[128,1024]{1,0:T(8,128)(2,1)S(1)}, bf16[128,1024]{1,0:T(8,128)(2,1)S(1)}, u32[]{:S(2)}, u32[]{:S(2)}) %collective-permute-start.1) | collective-permute-done | bytes 262176 | tf_op jit(solution)/shard_map/ppermute | solution.py:15
  80.3 1.9 %collective-permute-start.2 = (bf16[128,1024]{1,0:T(8,128)(2,1)S(1)}, bf16[128,1024]{1,0:T(8,128)(2,1)S(1)}, u32[]{:S(2)}, u32[]{:S(2)}) collective-permute-start(bf16[128,1024]{1,0:T(8,128)(2,1)S(1)} %collective-permute-done.1), channel_id=1, source_target_pairs={{0,8},{8,16},{16,24},{24,32},{32,40},{40,48},{48,56},{56,64},{64,7... | collective-permute-start | bytes 786440 | tf_op jit(solution)/shard_map/ppermute | solution.py:15
  82.2 0.6 convolution_negate_fusion.3
  82.8 0.6 fusion.83
  83.3 6.7 %collective-permute-done.2 = bf16[128,1024]{1,0:T(8,128)(2,1)S(1)} collective-permute-done((bf16[128,1024]{1,0:T(8,128)(2,1)S(1)}, bf16[128,1024]{1,0:T(8,128)(2,1)S(1)}, u32[]{:S(2)}, u32[]{:S(2)}) %collective-permute-start.2) | collective-permute-done | bytes 262176 | tf_op jit(solution)/shard_map/ppermute | solution.py:15
  90.1 1.9 %collective-permute-start.3 = (bf16[128,1024]{1,0:T(8,128)(2,1)S(1)}, bf16[128,1024]{1,0:T(8,128)(2,1)S(1)}, u32[]{:S(2)}, u32[]{:S(2)}) collective-permute-start(bf16[128,1024]{1,0:T(8,128)(2,1)S(1)} %collective-permute-done.2), channel_id=1, source_target_pairs={{0,8},{8,16},{16,24},{24,32},{32,40},{40,48},{48,56},{56,64},{64,7... | collective-permute-start | bytes 786440 | tf_op jit(solution)/shard_map/ppermute | solution.py:15
  92.0 0.6 convolution_negate_fusion.2
  92.6 0.6 fusion.81
  93.1 6.7 %collective-permute-done.3 = bf16[128,1024]{1,0:T(8,128)(2,1)S(1)} collective-permute-done((bf16[128,1024]{1,0:T(8,128)(2,1)S(1)}, bf16[128,1024]{1,0:T(8,128)(2,1)S(1)}, u32[]{:S(2)}, u32[]{:S(2)}) %collective-permute-start.3) | collective-permute-done | bytes 262176 | tf_op jit(solution)/shard_map/ppermute | solution.py:15
  99.9 0.6 convolution_negate_fusion.1
  100.4 0.6 fusion.79
  101.0 2.4 %fusion.23 = f32[128,1024]{1,0:T(8,128)S(1)} fusion(f32[256,1024]{1,0:T(8,128)S(1)} %convolution_negate_fusion.1, f32[256,1024]{1,0:T(8,128)S(1)} %fusion.79, f32[256,1024]{1,0:T(8,128)S(1)} %convolution_negate_fusion.2, f32[256,1024]{1,0:T(8,128)S(1)} %fusion.81, f32[256,1024]{1,0:T(8,128)S(1)} %convolution_negate_fusion.3, f32[256,1024]{1,0:T(8,128)S(1)} %fusion.83, ...), kind=kOutput, calls=%fused_computation.37 | convolution fusion | flops 407633920 | bytes 21626880 | tf_op jit(solution)/shard_map/dot_general | solution.py:19
  103.5 3.2 %fusion.3 = bf16[128,1024]{1,0:T(8,128)(2,1)} fusion(f32[128,1024]{1,0:T(8,128)S(1)} %fusion.23, f32[256,1024]{1,0:T(8,128)S(1)} %convolution_negate_fusion.1, f32[256,1024]{1,0:T(8,128)S(1)} %fusion.79, f32[256,1024]{1,0:T(8,128)S(1)} %convolution_negate_fusion.2, f32[256,1024]{1,0:T(8,128)S(1)} %fusion.81, f32[256,1024]{1,0:T(8,128)S(1)} %convolution_negate_fusion.3, ...), kind=kOutput, calls=%fused_computation.12 | convolution fusion | flops 408682496 | bytes 22417408 | tf_op jit(solution)/shard_map/dot_general | solution.py:19
  (10 shorter events, 0.2 us)
Async XLA Ops:
  50.6 19.8 %collective-permute-start = (bf16[128,1024]{1,0:T(8,128)(2,1)S(1)}, bf16[128,1024]{1,0:T(8,128)(2,1)S(1)}, u32[]{:S(2)}, u32[]{:S(2)}) collective-permute-start(bf16[128,1024]{1,0:T(8,128)(2,1)S(1)} %fusion.64), channel_id=1, source_target_pairs={{0,8},{8,16},{16,24},{24,32},{32,40},{40,48},{48,56},{56,64},{64,7... | collective-permute-start | bytes 786440 | tf_op jit(solution)/shard_map/ppermute | solution.py:15
  70.5 9.8 %collective-permute-start.1 = (bf16[128,1024]{1,0:T(8,128)(2,1)S(1)}, bf16[128,1024]{1,0:T(8,128)(2,1)S(1)}, u32[]{:S(2)}, u32[]{:S(2)}) collective-permute-start(bf16[128,1024]{1,0:T(8,128)(2,1)S(1)} %collective-permute-done), channel_id=1, source_target_pairs={{0,8},{8,16},{16,24},{24,32},{32,40},{40,48},{48,56},{56,64},{64,7... | collective-permute-start | bytes 786440 | tf_op jit(solution)/shard_map/ppermute | solution.py:15
  80.3 9.8 %collective-permute-start.2 = (bf16[128,1024]{1,0:T(8,128)(2,1)S(1)}, bf16[128,1024]{1,0:T(8,128)(2,1)S(1)}, u32[]{:S(2)}, u32[]{:S(2)}) collective-permute-start(bf16[128,1024]{1,0:T(8,128)(2,1)S(1)} %collective-permute-done.1), channel_id=1, source_target_pairs={{0,8},{8,16},{16,24},{24,32},{32,40},{40,48},{48,56},{56,64},{64,7... | collective-permute-start | bytes 786440 | tf_op jit(solution)/shard_map/ppermute | solution.py:15
  90.1 9.8 %collective-permute-start.3 = (bf16[128,1024]{1,0:T(8,128)(2,1)S(1)}, bf16[128,1024]{1,0:T(8,128)(2,1)S(1)}, u32[]{:S(2)}, u32[]{:S(2)}) collective-permute-start(bf16[128,1024]{1,0:T(8,128)(2,1)S(1)} %collective-permute-done.2), channel_id=1, source_target_pairs={{0,8},{8,16},{16,24},{24,32},{32,40},{40,48},{48,56},{56,64},{64,7... | collective-permute-start | bytes 786440 | tf_op jit(solution)/shard_map/ppermute | solution.py:15
  101.0 2.5 %copy-start = (bf16[128,1024]{1,0:T(8,128)(2,1)S(1)}, bf16[128,1024]{1,0:T(8,128)(2,1)}, u32[]{:S(2)}) copy-start(bf16[128,1024]{1,0:T(8,128)(2,1)} %param.5) | copy-start | bytes 786436
  101.0 2.5 %copy-start.1 = (f32[1024]{0:T(1024)S(1)}, f32[1024]{0:T(1024)}, u32[]{:S(2)}) copy-start(f32[1024]{0:T(1024)} %param.7) | copy-start | bytes 12292
where the time goes:
time: 107 us
  blocking collectives  48.5 us (45%)
  matrix products  23.8 us (22%)
  waiting for transfers between devices  18.6 us (17%)
  starting transfers between devices  9.32 us (9%)
  other arithmetic  6.35 us (6%)
    psum x1, blocking collectives, on_device(): square_sum = lax.psum(jnp.sum(values * values, axis=1), 'chan')  48.5 us
    dot_general x14, matrix products, product_hi(): jnp.dot(left, right, precision=lax.Precision.HIGHEST, preferred_element_t...  23.8 us
    ppermute x4, waiting for transfers between devices, passed_along(): lax.ppermute(value, axis, [(source, source + steps) for source in range(l...  18.6 us
    ppermute x4, starting transfers between devices, passed_along(): lax.ppermute(value, axis, [(source, source + steps) for source in range(l...  9.32 us
  transfers between devices with their start and end apart: 4, of which 3 were waited for; matrix products, arithmetic and copies ran while one was open for 20% of the time, Pallas kernels for 0%

commit v1 on v0

v1 whole, which is shorter than its diff:
```python
import math

import jax
import jax.numpy as jnp
import numpy as np
from jax import lax
from jax.experimental import pallas as pl
from jax.experimental.pallas import tpu as pltpu
from jax.sharding import PartitionSpec as P

D = 8192
MESH = pl.DeviceIdType.MESH
B = 128
LAGS = 4
RING = 128
FAR = 32
CW = 256
CHUNKS = 4
ROWS = B // CHUNKS


def split(value):
    hi = value.astype(jnp.bfloat16)
    return hi, (value - hi.astype(jnp.float32)).astype(jnp.bfloat16)


def tables():
    bins = np.concatenate([np.arange(0, B, 2), np.arange(1, B, 2)])
    angle = np.pi * np.outer(2 * bins + 1, np.arange(B)) / (2 * B)
    forward = np.concatenate([np.cos(angle), -np.sin(angle)], 0)
    inverse = forward.T / B

    def halves(table):
        table = table.astype(np.float32)
        hi = table.astype(jnp.bfloat16)
        lo = (table - hi.astype(np.float32)).astype(jnp.bfloat16)
        return np.concatenate([hi, lo], 1)

    return forward.astype(np.float32), halves(forward), halves(inverse)


def kernel(
    x_hbm,
    gate_hbm,
    taps_hbm,
    skip_hbm,
    ftab_hbm,
    fcat_hbm,
    icat_hbm,
    out,
    xv,
    gate,
    taps,
    skip,
    ftab,
    fcat,
    icat,
    halo,
    spec,
    fs,
    part,
    xpart,
    zsum,
    zpart,
    total,
    ytotal,
    load_sem,
    own_send,
    fwd_send,
    mate_send,
    halo_recv,
    x_send,
    x_recv,
    z_send,
    z_recv,
    y_send,
    y_recv,
):
    seq, chan = lax.axis_index("seq"), lax.axis_index("chan")
    half, col = lax.div(chan, 4), lax.rem(chan, 4)
    place = half * 64 + seq
    odd = lax.rem(place, 2) == 1

    def at(shift):
        spot = lax.rem(place + (shift + RING), RING)
        return (lax.rem(spot, 64), lax.div(spot, 64) * 4 + col)

    def beside(shift):
        return (seq, half * 4 + lax.rem(col + shift, 4))

    loads = [
        pltpu.make_async_copy(src, dst, load_sem.at[n])
        for n, (src, dst) in enumerate(
            [
                (x_hbm, xv),
                (fcat_hbm, fcat),
                (taps_hbm, taps),
                (skip_hbm, skip),
                (ftab_hbm, ftab),
                (icat_hbm, icat),
                (gate_hbm, gate),
            ]
        )
    ]
    for load in loads:
        load.start()

    barrier = pltpu.get_barrier_semaphore()
    peers = [beside(d) for d in (1, 2, 3)]
    peers += [at(d) for k in (1, 2, 3, 4, FAR) for d in (k, -k)]
    for peer in peers:
        pl.semaphore_signal(barrier, inc=1, device_id=peer, device_id_type=MESH)
    pl.semaphore_wait(barrier, len(peers))

    def remote(src, dst, send, recv, device):
        return pltpu.make_async_remote_copy(
            src_ref=src,
            dst_ref=dst,
            send_sem=send,
            recv_sem=recv,
            device_id=device,
            device_id_type=MESH,
        )

    def piece(n):
        return pl.ds(n * ROWS, ROWS)

    mate = lax.rem(place, 2) * -2 + 1

    def to_next(src, slot, n, send):
        return remote(
            src.at[piece(n)], halo.at[slot, piece(n)], send.at[n], halo_recv.at[slot, n], at(2)
        )

    def to_mate(src, slot, n):
        return remote(
            src.at[piece(n)],
            halo.at[slot, piece(n)],
            mate_send.at[slot // 2, n],
            halo_recv.at[slot, n],
            at(mate),
        )

    own = [to_next(x_hbm, 1, n, own_send) for n in range(CHUNKS)]
    for copy in own:
        copy.start()

    @pl.when(jnp.logical_not(odd))
    def _():
        for n in range(CHUNKS):
            to_mate(x_hbm, 0, n).start()

    loads[0].wait()
    gram = lax.dot_general(
        xv[...], xv[...], (((1,), (1,)), ((), ())), preferred_element_type=jnp.float32
    )
    diagonal = lax.broadcasted_iota(jnp.int32, (B, B), 0) == lax.broadcasted_iota(
        jnp.int32, (B, B), 1
    )
    part[...] = jnp.sum(jnp.where(diagonal, gram, 0.0), axis=0, keepdims=True)
    xs = [
        remote(part, xpart.at[d - 1], x_send.at[d - 1], x_recv.at[d - 1], beside(d))
        for d in (1, 2, 3)
    ]
    for copy in xs:
        copy.start()

    for load in loads[1:]:
        load.wait()

    def filter_spectra(step, carry):
        cols = pl.ds(pl.multiple_of(step * CW, CW), CW)
        last_re = last_im = None
        for lag in range(LAGS + 1):
            if lag < LAGS:
                block = taps[lag * B : (lag + 1) * B, cols]
                here = jnp.dot(
                    fcat[...],
                    jnp.concatenate([block, block], 0),
                    preferred_element_type=jnp.float32,
                )
                re, im = here[:B], here[B:]
                if lag == 0:
                    full_re, full_im = re + skip[:, cols], im
                else:
                    full_re, full_im = re, im
            else:
                full_re = jnp.broadcast_to(taps[LAGS * B : LAGS * B + 1, cols].astype(jnp.float32), (B, CW))
                full_im = None
            if last_re is not None:
                h = B // 2
                full_re = jnp.concatenate(
                    [full_re[:h] - last_im[:h], full_re[h:] + last_im[h:]], 0
                )
                if full_im is None:
                    full_im = jnp.concatenate([last_re[:h], -last_re[h:]], 0)
                else:
                    full_im = jnp.concatenate(
                        [full_im[:h] + last_re[:h], full_im[h:] - last_re[h:]], 0
                    )
            spec[lag, :B, cols] = full_re
            spec[lag, B:, cols] = full_im
            if lag < LAGS:
                last_re, last_im = re, im
        return carry

    steps = xv.shape[1] // CW
    lax.fori_loop(0, steps // 2, filter_spectra, 0)

    for copy in xs:
        copy.wait_recv()
    zsum[...] = part[...] + xpart[0] + xpart[1] + xpart[2]
    first_leg = remote(zsum, zpart.at[0], z_send.at[0], z_recv.at[0], at(FAR))
    first_leg.start()

    lax.fori_loop(steps // 2, steps, filter_spectra, 0)

    def forward(n):
        own[n].wait_recv()
        to_next(halo.at[1], 3, n, fwd_send).start()

        @pl.when(odd)
        def _():
            to_mate(halo.at[1], 0, n).start()

        @pl.when(jnp.logical_not(odd))
        def _():
            to_mate(halo.at[1], 2, n).start()

    forward(0)
    forward(1)
    first_leg.wait_recv()
    second_leg = remote(zpart.at[0], zpart.at[1], z_send.at[1], z_recv.at[1], at(FAR))
    second_leg.start()
    forward(2)
    forward(3)
    second_leg.wait_recv()
    total[...] = zsum[...] + zpart[1]
    ys = [
        remote(total, ytotal.at[k - 1], y_send.at[k - 1], y_recv.at[k - 1], at(k))
        for k in range(1, LAGS + 1)
    ]
    for copy in ys:
        copy.start()

    def scaled(lag, sums):
        scale = lax.rsqrt(sums * (1.0 / D) + 1e-06)
        scale = jnp.where(seq >= lag, scale, 0.0)
        hi, lo = split(ftab[...] * scale)
        fs[lag, :, :B] = hi
        fs[lag, :, B:] = lo

    scaled(0, total[...])

    fwd = [to_next(halo.at[1], 3, n, fwd_send) for n in range(CHUNKS)]
    for n in range(CHUNKS):
        fwd[n].wait_recv()

        @pl.when(odd)
        def _():
            to_mate(halo.at[3], 2, n).start()

    for k in range(1, LAGS + 1):
        ys[k - 1].wait_recv()
        scaled(k, ytotal[k - 1])
    for n in range(CHUNKS):
        to_mate(halo.at[1], 0, n).wait_recv()
        to_mate(halo.at[1], 2, n).wait_recv()

    def convolve(step, carry):
        cols = pl.ds(pl.multiple_of(step * CW, CW), CW)
        acc_re = acc_im = None
        for lag in range(LAGS + 1):
            block = xv[:, cols] if lag == 0 else halo[lag - 1, :, cols]
            here = jnp.dot(
                fs[lag],
                jnp.concatenate([block, block], 0),
                preferred_element_type=jnp.float32,
            )
            re, im = here[:B], here[B:]
            sre, sim = spec[lag, :B, cols], spec[lag, B:, cols]
            pre, pim = re * sre - im * sim, re * sim + im * sre
            acc_re = pre if lag == 0 else acc_re + pre
            acc_im = pim if lag == 0 else acc_im + pim
        hi, lo = split(jnp.concatenate([acc_re, acc_im], 0))
        ihi, ilo = icat[:, : 2 * B], icat[:, 2 * B :]
        result = (
            jnp.dot(ihi, hi, preferred_element_type=jnp.float32)
            + jnp.dot(ihi, lo, preferred_element_type=jnp.float32)
            + jnp.dot(ilo, hi, preferred_element_type=jnp.float32)
        )
        out[:, cols] = (gate[:, cols].astype(jnp.float32) * result).astype(jnp.bfloat16)
        return carry

    lax.fori_loop(0, steps, convolve, 0)

    for copy in own + fwd + xs + [first_leg, second_leg] + ys:
        copy.wait_send()
    for n in range(CHUNKS):
        to_mate(halo.at[1], 0, n).wait_send()
        to_mate(halo.at[1], 2, n).wait_send()


def on_device(inputs, gating, long_filter, skip_scale):
    rows, channels = inputs.shape
    bf16, f32 = jnp.bfloat16, jnp.float32
    ftab, fcat, icat = tables()
    dma = pltpu.SemaphoreType.DMA
    return pl.pallas_call(
        kernel,
        out_shape=jax.ShapeDtypeStruct((rows, channels), bf16),
        in_specs=[pl.BlockSpec(memory_space=pltpu.HBM)] * 7,
        out_specs=pl.BlockSpec(memory_space=pltpu.VMEM),
        scratch_shapes=[
            pltpu.VMEM((rows, channels), bf16),
            pltpu.VMEM((rows, channels), bf16),
            pltpu.VMEM(long_filter.shape, bf16),
            pltpu.VMEM((1, channels), f32),
            pltpu.VMEM(ftab.shape, f32),
            pltpu.VMEM(fcat.shape, bf16),
            pltpu.VMEM(icat.shape, bf16),
            pltpu.VMEM((LAGS, rows, channels), bf16),
            pltpu.VMEM((LAGS + 1, 2 * B, channels), f32),
            pltpu.VMEM((LAGS + 1, 2 * B, 2 * B), bf16),
            pltpu.VMEM((1, B), f32),
            pltpu.VMEM((3, 1, B), f32),
            pltpu.VMEM((1, B), f32),
            pltpu.VMEM((2, 1, B), f32),
            pltpu.VMEM((1, B), f32),
            pltpu.VMEM((LAGS, 1, B), f32),
            dma((7,)),
            dma((CHUNKS,)),
            dma((CHUNKS,)),
            dma((2, CHUNKS)),
            dma((LAGS, CHUNKS)),
            dma((3,)),
            dma((3,)),
            dma((2,)),
            dma((2,)),
            dma((LAGS,)),
            dma((LAGS,)),
        ],
        compiler_params=pltpu.CompilerParams(
            collective_id=0, has_side_effects=True, vmem_limit_bytes=60 * 1024 * 1024
        ),
    )(inputs, gating, long_filter, skip_scale[None, :], ftab, fcat, icat)


def solution(mesh):
    in_specs = (P("seq", "chan"), P("seq", "chan"), P(None, "chan"), P("chan"))
    return jax.shard_map(
        on_device, mesh=mesh, in_specs=in_specs, out_specs=P("seq", "chan"), check_vma=False
    )
```

time: 107 us -> 39.6 us (0.37)
  the two profiles are of different devices: /device:TPU:32 before, /device:TPU:1 now
where the time goes in v1:
time: 39.6 us; the launch traced here: 39.5 us
  Pallas kernels  37.8 us (95%)
  local copies, waits for them, and re-layouts  1.67 us (4%)
    pallas_call x1, Pallas kernels, on_device(): pl.pallas_call(kernel, out_shape=jax.ShapeDtypeStruct((rows, channels), b...  37.8 us
    unnamed x1, local copies, waits for them, and re-layouts  1.67 us

profile of v1, /device:TPU:1, one launch (start us, length us, event | category | flops | bytes accessed | tf_op | source)
XLA Modules:
  0.0 39.5 jit_solution(3721897762863829977)
XLA Ops:
  0.0 37.8 %shard_map.73 = bf16[128,1024]{1,0:T(8,128)(2,1)} custom-call(bf16[128,1024]{1,0:T(8,128)(2,1)} %x_hbm.1, bf16[128,1024]{1,0:T(8,128)(2,1)} %gate_hbm.1, bf16[513,1024]{1,0:T(8,128)(2,1)} %taps_hbm.1, f32[1,1024]{1,0:T(1,128)} %bitcast.1, f32[256,128]{1,0:T(8,128)} %constant.6.clone.ftab_hbm, bf16[256,256]{1,0:T(8,128)(2,1)} %constant.7.clone.fcat_hbm, ...), custom_call_target="tpu_custom_call" | custom-call | tf_op jit(solution)/shard_map/pallas_call | solution.py:309
  37.8 1.7 %copy.9 = bf16[128,1024]{1,0:T(8,128)(2,1)} copy(bf16[128,1024]{1,0:T(8,128)(2,1)} %shard_map.73) | data formatting | bytes 524288

commit v2 on v1

v2 whole, which is shorter than its diff:
```python
import functools

import jax
import jax.numpy as jnp
import numpy as np
from jax import lax
from jax.experimental import pallas as pl
from jax.experimental.pallas import tpu as pltpu
from jax.sharding import PartitionSpec as P

D = 8192
MESH = pl.DeviceIdType.MESH
B = 128
LAGS = 4
CW = 256
CHUNKS = 4
ROWS = B // CHUNKS


def split(value):
    hi = value.astype(jnp.bfloat16)
    return hi, (value - hi.astype(jnp.float32)).astype(jnp.bfloat16)


def tables():
    bins = np.concatenate([np.arange(0, B, 2), np.arange(1, B, 2)])
    angle = np.pi * np.outer(2 * bins + 1, np.arange(B)) / (2 * B)
    forward = np.concatenate([np.cos(angle), -np.sin(angle)], 0)
    inverse = forward.T / B

    def halves(table):
        table = table.astype(np.float32)
        hi = table.astype(jnp.bfloat16)
        lo = (table - hi.astype(np.float32)).astype(jnp.bfloat16)
        return np.concatenate([hi, lo], 1)

    return forward.astype(np.float32), halves(forward), halves(inverse)


def kernel(
    x_hbm,
    gate_hbm,
    taps_hbm,
    skip_hbm,
    ftab_hbm,
    fcat_hbm,
    icat_hbm,
    out,
    xv,
    gate,
    taps,
    skip,
    ftab,
    fcat,
    icat,
    halo,
    spec,
    acc,
    part,
    xpart,
    xsum,
    near,
    away,
    load_sem,
    own_send,
    fwd_send,
    mate_send,
    halo_recv,
    x_send,
    x_recv,
    near_send,
    near_recv,
    away_send,
    away_recv,
    ready,
):
    seq, chan = lax.axis_index("seq"), lax.axis_index("chan")
    count = lax.axis_size("seq")
    half, col = lax.div(chan, 4), lax.rem(chan, 4)
    upper = half == 1
    odd = lax.rem(seq, 2) == 1
    even = jnp.logical_not(odd)
    lags = range(1, LAGS + 1)
    spans = range(LAGS + 1)

    def ahead(k):
        return (seq + k, chan)

    def across(k):
        return (seq + k, (1 - half) * 4 + col)

    def beside(shift):
        return (seq, half * 4 + lax.rem(col + shift, 4))

    def has(k):
        return jnp.logical_and(seq + k >= 0, seq + k < count)

    def signal(sem, device):
        pl.semaphore_signal(sem, inc=1, device_id=device, device_id_type=MESH)

    loads = [
        pltpu.make_async_copy(src, dst, load_sem.at[n])
        for n, (src, dst) in enumerate(
            [
                (x_hbm, xv),
                (fcat_hbm, fcat),
                (taps_hbm, taps),
                (skip_hbm, skip),
                (ftab_hbm, ftab),
                (icat_hbm, icat),
                (gate_hbm, gate),
            ]
        )
    ]

    barrier = pltpu.get_barrier_semaphore()
    for k in lags:
        pl.when(has(-k))(functools.partial(signal, barrier, ahead(-k)))
    pl.when(even)(functools.partial(signal, barrier, ahead(1)))
    for shift in (1, 2, 3):
        signal(barrier, beside(shift))

    @pl.when(jnp.logical_not(upper))
    def _():
        for k in range(-LAGS, LAGS + 1):
            pl.when(has(k))(functools.partial(signal, barrier, across(k)))

    for load in loads:
        load.start()

    before, after = jnp.minimum(seq, LAGS), jnp.minimum(count - 1 - seq, LAGS)
    pl.semaphore_wait(barrier, 3 + after + lax.rem(seq, 2) + half * (before + after + 1))

    @pl.when(upper)
    def _():
        for k in spans:
            pl.when(has(-k))(functools.partial(signal, ready, across(-k)))

    def remote(src, dst, send, recv, device):
        return pltpu.make_async_remote_copy(
            src_ref=src,
            dst_ref=dst,
            send_sem=send,
            recv_sem=recv,
            device_id=device,
            device_id_type=MESH,
        )

    def piece(n):
        return pl.ds(n * ROWS, ROWS)

    def to_next(src, slot, n, send):
        return remote(
            src.at[piece(n)], halo.at[slot, piece(n)], send.at[n], halo_recv.at[slot, n], ahead(2)
        )

    def to_mate(src, slot, n):
        return remote(
            src.at[piece(n)],
            halo.at[slot, piece(n)],
            mate_send.at[slot // 2, n],
            halo_recv.at[slot, n],
            ahead(1 - 2 * lax.rem(seq, 2)),
        )

    pieces = range(CHUNKS)
    own = [to_next(x_hbm, 1, n, own_send) for n in pieces]
    onward = [to_next(halo.at[1], 3, n, fwd_send) for n in pieces]
    even_first = [to_mate(x_hbm, 0, n) for n in pieces]
    even_second = [to_mate(halo.at[1], 2, n) for n in pieces]
    odd_first = [to_mate(halo.at[1], 0, n) for n in pieces]
    odd_second = [to_mate(halo.at[3], 2, n) for n in pieces]

    def each(copies, act):
        for copy in copies:
            act(copy)

    @pl.when(has(2))
    def _():
        each(own, lambda copy: copy.start())

    loads[0].wait()
    gram = lax.dot_general(
        xv[...], xv[...], (((1,), (1,)), ((), ())), preferred_element_type=jnp.float32
    )
    diagonal = lax.broadcasted_iota(jnp.int32, (B, B), 0) == lax.broadcasted_iota(
        jnp.int32, (B, B), 1
    )
    part[...] = jnp.sum(jnp.where(diagonal, gram, 0.0), axis=0, keepdims=True)
    xs = [
        remote(part, xpart.at[d - 1], x_send.at[d - 1], x_recv.at[d - 1], beside(d))
        for d in (1, 2, 3)
    ]
    each(xs, lambda copy: copy.start())

    @pl.when(even)
    def _():
        each(even_first, lambda copy: copy.start())

    for k in lags:

        @pl.when(seq < k)
        def _():
            halo[k - 1] = jnp.zeros(halo.shape[1:], halo.dtype)

    each(loads[1:4], lambda copy: copy.wait())

    def filter_spectra(step, carry):
        cols = pl.ds(pl.multiple_of(step * CW, CW), CW)
        last_re = last_im = None
        for lag in spans:
            if lag < LAGS:
                block = taps[lag * B : (lag + 1) * B, cols]
                here = jnp.dot(
                    fcat[...],
                    jnp.concatenate([block, block], 0),
                    preferred_element_type=jnp.float32,
                )
                re, im = here[:B], here[B:]
                full_re, full_im = (re + skip[:, cols] if lag == 0 else re), im
            else:
                tap = taps[LAGS * B : LAGS * B + 1, cols].astype(jnp.float32)
                full_re, full_im = jnp.broadcast_to(tap, (B, CW)), jnp.zeros((B, CW), jnp.float32)
            if last_re is not None:
                h = B // 2
                turned_re = jnp.concatenate([-last_im[:h], last_im[h:]], 0)
                turned_im = jnp.concatenate([last_re[:h], -last_re[h:]], 0)
                full_re, full_im = full_re + turned_re, full_im + turned_im
            spec[lag, :B, cols] = full_re
            spec[lag, B:, cols] = full_im
            if lag < LAGS:
                last_re, last_im = re, im
        return carry

    steps = xv.shape[1] // CW
    lax.fori_loop(0, steps // 2, filter_spectra, 0)

    each(xs, lambda copy: copy.wait_recv())
    xsum[...] = part[...] + xpart[0] + xpart[1] + xpart[2]
    nears = [
        remote(xsum, near.at[k - 1], near_send.at[k - 1], near_recv.at[k - 1], ahead(k))
        for k in lags
    ]
    aways = [
        remote(xsum, away.at[k], away_send.at[k], away_recv.at[k], across(k)) for k in spans
    ]

    def send_away():
        for k in spans:
            pl.when(has(k))(lambda copy=aways[k]: copy.start())

    pl.when(upper)(send_away)
    for k in lags:
        pl.when(has(k))(lambda copy=nears[k - 1]: copy.start())

    lax.fori_loop(steps // 2, steps, filter_spectra, 0)

    @pl.when(has(-2))
    def _():
        for n in pieces:
            own[n].wait_recv()
            pl.when(has(2))(lambda n=n: onward[n].start())
            pl.when(odd)(lambda n=n: odd_first[n].start())
            pl.when(even)(lambda n=n: even_second[n].start())

    @pl.when(jnp.logical_not(upper))
    def _():
        pl.semaphore_wait(ready, after + 1)
        send_away()

    @pl.when(has(-4))
    def _():
        for n in pieces:
            onward[n].wait_recv()
            pl.when(odd)(lambda n=n: odd_second[n].start())

    each(loads[4:], lambda copy: copy.wait())

    def scaled(lag):
        if lag == 0:
            sums = xsum[...] + away[0]
        else:
            sums = near[lag - 1] + away[lag]
        scale = lax.rsqrt(sums * (1.0 / D) + 1e-06)
        if lag:
            scale = jnp.where(seq >= lag, scale, 0.0)
        return jnp.concatenate(split(ftab[...] * scale), 1)

    def arrived(lag):
        if lag in (1, 3):
            each(odd_first if lag == 1 else odd_second, lambda copy: copy.wait_recv())
        nears[lag - 1].wait_recv()
        aways[lag].wait_recv()

    for lag in spans:
        if lag == 0:
            aways[0].wait_recv()
        else:
            pl.when(seq >= lag)(functools.partial(arrived, lag))
        table = scaled(lag)

        def convolve(step, carry, lag=lag, table=table):
            cols = pl.ds(pl.multiple_of(step * CW, CW), CW)
            block = xv[:, cols] if lag == 0 else halo[lag - 1, :, cols]
            here = jnp.dot(
                table, jnp.concatenate([block, block], 0), preferred_element_type=jnp.float32
            )
            re, im = here[:B], here[B:]
            sre, sim = spec[lag, :B, cols], spec[lag, B:, cols]
            new_re, new_im = re * sre - im * sim, re * sim + im * sre
            if lag:
                new_re, new_im = new_re + acc[:B, cols], new_im + acc[B:, cols]
            if lag < LAGS:
                acc[:B, cols] = new_re
                acc[B:, cols] = new_im
                return carry
            hi, lo = split(jnp.concatenate([new_re, new_im], 0))
            ihi, ilo = icat[:, : 2 * B], icat[:, 2 * B :]
            result = (
                jnp.dot(ihi, hi, preferred_element_type=jnp.float32)
                + jnp.dot(ihi, lo, preferred_element_type=jnp.float32)
                + jnp.dot(ilo, hi, preferred_element_type=jnp.float32)
            )
            out[:, cols] = (gate[:, cols].astype(jnp.float32) * result).astype(jnp.bfloat16)
            return carry

        lax.fori_loop(0, steps, convolve, 0)

    each(xs, lambda copy: copy.wait_send())
    for k in spans:
        pl.when(has(k))(lambda copy=aways[k]: copy.wait_send())
    for k in lags:
        pl.when(has(k))(lambda copy=nears[k - 1]: copy.wait_send())

    def sent(copies):
        each(copies, lambda copy: copy.wait_send())

    pl.when(has(2))(lambda: sent(own))
    pl.when(jnp.logical_and(has(2), has(-2)))(lambda: sent(onward))
    pl.when(even)(lambda: sent(even_first))
    pl.when(jnp.logical_and(even, has(-2)))(lambda: sent(even_second))
    pl.when(jnp.logical_and(odd, has(-2)))(lambda: sent(odd_first))
    pl.when(jnp.logical_and(odd, has(-4)))(lambda: sent(odd_second))


def on_device(inputs, gating, long_filter, skip_scale):
    rows, channels = inputs.shape
    bf16, f32 = jnp.bfloat16, jnp.float32
    ftab, fcat, icat = tables()
    dma = pltpu.SemaphoreType.DMA
    return pl.pallas_call(
        kernel,
        out_shape=jax.ShapeDtypeStruct((rows, channels), bf16),
        in_specs=[pl.BlockSpec(memory_space=pltpu.HBM)] * 7,
        out_specs=pl.BlockSpec(memory_space=pltpu.VMEM),
        scratch_shapes=[
            pltpu.VMEM((rows, channels), bf16),
            pltpu.VMEM((rows, channels), bf16),
            pltpu.VMEM(long_filter.shape, bf16),
            pltpu.VMEM((1, channels), f32),
            pltpu.VMEM(ftab.shape, f32),
            pltpu.VMEM(fcat.shape, bf16),
            pltpu.VMEM(icat.shape, bf16),
            pltpu.VMEM((LAGS, rows, channels), bf16),
            pltpu.VMEM((LAGS + 1, 2 * B, channels), f32),
            pltpu.VMEM((2 * B, channels), f32),
            pltpu.VMEM((1, B), f32),
            pltpu.VMEM((3, 1, B), f32),
            pltpu.VMEM((1, B), f32),
            pltpu.VMEM((LAGS, 1, B), f32),
            pltpu.VMEM((LAGS + 1, 1, B), f32),
            dma((7,)),
            dma((CHUNKS,)),
            dma((CHUNKS,)),
            dma((2, CHUNKS)),
            dma((LAGS, CHUNKS)),
            dma((3,)),
            dma((3,)),
            dma((LAGS,)),
            dma((LAGS,)),
            dma((LAGS + 1,)),
            dma((LAGS + 1,)),
            pltpu.SemaphoreType.REGULAR,
        ],
        compiler_params=pltpu.CompilerParams(
            collective_id=0, has_side_effects=True, vmem_limit_bytes=60 * 1024 * 1024
        ),
    )(inputs, gating, long_filter, skip_scale[None, :], ftab, fcat, icat)


def solution(mesh):
    in_specs = (P("seq", "chan"), P("seq", "chan"), P(None, "chan"), P("chan"))
    return jax.shard_map(
        on_device, mesh=mesh, in_specs=in_specs, out_specs=P("seq", "chan"), check_vma=False
    )
```

time: 39.6 us -> 33.4 us (0.84)
  the two profiles are of different devices: /device:TPU:1 before, /device:TPU:24 now
where the time goes in v2:
time: 33.4 us; the launch traced here: 33.2 us
  Pallas kernels  31.6 us (95%)
  local copies, waits for them, and re-layouts  1.67 us (5%)
    pallas_call x1, Pallas kernels, on_device(): pl.pallas_call(kernel, out_shape=jax.ShapeDtypeStruct((rows, channels), b...  31.6 us
    unnamed x1, local copies, waits for them, and re-layouts  1.67 us

profile of v2, /device:TPU:24, one launch (start us, length us, event | category | flops | bytes accessed | tf_op | source)
XLA Modules:
  0.0 33.2 jit_solution(7564308845796231996)
XLA Ops:
  0.0 31.6 %shard_map.73 = bf16[128,1024]{1,0:T(8,128)(2,1)} custom-call(bf16[128,1024]{1,0:T(8,128)(2,1)} %x_hbm.1, bf16[128,1024]{1,0:T(8,128)(2,1)} %gate_hbm.1, bf16[513,1024]{1,0:T(8,128)(2,1)} %taps_hbm.1, f32[1,1024]{1,0:T(1,128)} %bitcast.1, f32[256,128]{1,0:T(8,128)} %constant.6.clone.ftab_hbm, bf16[256,256]{1,0:T(8,128)(2,1)} %constant.7.clone.fcat_hbm, ...), custom_call_target="tpu_custom_call" | custom-call | tf_op jit(solution)/shard_map/pallas_call | solution.py:351
  31.6 1.7 %copy.9 = bf16[128,1024]{1,0:T(8,128)(2,1)} copy(bf16[128,1024]{1,0:T(8,128)(2,1)} %shard_map.73) | data formatting | bytes 524288

commit v3 on v2

--- a/solution.py
+++ b/solution.py
@@ -13,6 +13,7 @@
 B = 128
 LAGS = 4
 CW = 256
+WIDE = 512
 CHUNKS = 4
 ROWS = B // CHUNKS
 
@@ -45,7 +46,7 @@
     ftab_hbm,
     fcat_hbm,
     icat_hbm,
-    out,
+    out_hbm,
     xv,
     gate,
     taps,
@@ -55,7 +56,8 @@
     icat,
     halo,
     spec,
-    acc,
+    fs,
+    out,
     part,
     xpart,
     xsum,
@@ -73,6 +75,8 @@
     away_send,
     away_recv,
     ready,
+    go,
+    out_sem,
 ):
     seq, chan = lax.axis_index("seq"), lax.axis_index("chan")
     count = lax.axis_size("seq")
@@ -113,28 +117,32 @@
         )
     ]
 
+    loads[0].start()
     barrier = pltpu.get_barrier_semaphore()
-    for k in lags:
-        pl.when(has(-k))(functools.partial(signal, barrier, ahead(-k)))
-    pl.when(even)(functools.partial(signal, barrier, ahead(1)))
     for shift in (1, 2, 3):
         signal(barrier, beside(shift))
+    for k in lags:
+        pl.when(has(k))(functools.partial(signal, barrier, ahead(k)))
 
     @pl.when(jnp.logical_not(upper))
     def _():
         for k in range(-LAGS, LAGS + 1):
             pl.when(has(k))(functools.partial(signal, barrier, across(k)))
 
-    for load in loads:
+    for load in loads[1:]:
         load.start()
 
+    loads[0].wait()
+    gram = lax.dot_general(
+        xv[...], xv[...], (((1,), (1,)), ((), ())), preferred_element_type=jnp.float32
+    )
+    diagonal = lax.broadcasted_iota(jnp.int32, (B, B), 0) == lax.broadcasted_iota(
+        jnp.int32, (B, B), 1
+    )
+    part[...] = jnp.sum(jnp.where(diagonal, gram, 0.0), axis=0, keepdims=True)
+
     before, after = jnp.minimum(seq, LAGS), jnp.minimum(count - 1 - seq, LAGS)
-    pl.semaphore_wait(barrier, 3 + after + lax.rem(seq, 2) + half * (before + after + 1))
-
-    @pl.when(upper)
-    def _():
-        for k in spans:
-            pl.when(has(-k))(functools.partial(signal, ready, across(-k)))
+    pl.semaphore_wait(barrier, 3 + before + half * (before + after + 1))
 
     def remote(src, dst, send, recv, device):
         return pltpu.make_async_remote_copy(
@@ -175,27 +183,19 @@
         for copy in copies:
             act(copy)
 
-    @pl.when(has(2))
-    def _():
-        each(own, lambda copy: copy.start())
-
-    loads[0].wait()
-    gram = lax.dot_general(
-        xv[...], xv[...], (((1,), (1,)), ((), ())), preferred_element_type=jnp.float32
-    )
-    diagonal = lax.broadcasted_iota(jnp.int32, (B, B), 0) == lax.broadcasted_iota(
-        jnp.int32, (B, B), 1
-    )
-    part[...] = jnp.sum(jnp.where(diagonal, gram, 0.0), axis=0, keepdims=True)
     xs = [
         remote(part, xpart.at[d - 1], x_send.at[d - 1], x_recv.at[d - 1], beside(d))
         for d in (1, 2, 3)
     ]
     each(xs, lambda copy: copy.start())
 
-    @pl.when(even)
-    def _():
-        each(even_first, lambda copy: copy.start())
+    for k in (2, 1, 3, 4):
+        pl.when(has(-k))(functools.partial(signal, go.at[k - 1], ahead(-k)))
+
+    @pl.when(upper)
+    def _():
+        for k in spans:
+            pl.when(has(-k))(functools.partial(signal, ready, across(-k)))
 
     for k in lags:
 
@@ -233,7 +233,20 @@
         return carry
 
     steps = xv.shape[1] // CW
-    lax.fori_loop(0, steps // 2, filter_spectra, 0)
+    lax.fori_loop(0, steps, filter_spectra, 0)
+
+    @pl.when(has(2))
+    def _():
+        pl.semaphore_wait(go.at[1], 1)
+        each(own, lambda copy: copy.start())
+
+    @pl.when(has(1))
+    def _():
+        pl.semaphore_wait(go.at[0], 1)
+
+        @pl.when(even)
+        def _():
+            each(even_first, lambda copy: copy.start())
 
     each(xs, lambda copy: copy.wait_recv())
     xsum[...] = part[...] + xpart[0] + xpart[1] + xpart[2]
@@ -251,9 +264,12 @@
 
     pl.when(upper)(send_away)
     for k in lags:
-        pl.when(has(k))(lambda copy=nears[k - 1]: copy.start())
-
-    lax.fori_loop(steps // 2, steps, filter_spectra, 0)
+
+        @pl.when(has(k))
+        def _():
+            if k > 2:
+                pl.semaphore_wait(go.at[k - 1], 1)
+            nears[k - 1].start()
 
     @pl.when(has(-2))
     def _():
@@ -284,7 +300,9 @@
         scale = lax.rsqrt(sums * (1.0 / D) + 1e-06)
         if lag:
             scale = jnp.where(seq >= lag, scale, 0.0)
-        return jnp.concatenate(split(ftab[...] * scale), 1)
+        hi, lo = split(ftab[...] * scale)
+        fs[lag, :, :B] = hi
+        fs[lag, :, B:] = lo
 
     def arrived(lag):
         if lag in (1, 3):
@@ -292,40 +310,46 @@
         nears[lag - 1].wait_recv()
         aways[lag].wait_recv()
 
+    def leave(step):
+        cols = pl.ds(pl.multiple_of(step * WIDE, WIDE), WIDE)
+        return pltpu.make_async_copy(out.at[:, cols], out_hbm.at[:, cols], out_sem.at[step])
+
     for lag in spans:
         if lag == 0:
             aways[0].wait_recv()
         else:
             pl.when(seq >= lag)(functools.partial(arrived, lag))
-        table = scaled(lag)
-
-        def convolve(step, carry, lag=lag, table=table):
-            cols = pl.ds(pl.multiple_of(step * CW, CW), CW)
+        scaled(lag)
+
+    def convolve(step, carry):
+        cols = pl.ds(pl.multiple_of(step * WIDE, WIDE), WIDE)
+        acc_re = acc_im = None
+        for lag in spans:
             block = xv[:, cols] if lag == 0 else halo[lag - 1, :, cols]
             here = jnp.dot(
-                table, jnp.concatenate([block, block], 0), preferred_element_type=jnp.float32
+                fs[lag], jnp.concatenate([block, block], 0), preferred_element_type=jnp.float32
             )
             re, im = here[:B], here[B:]
             sre, sim = spec[lag, :B, cols], spec[lag, B:, cols]
             new_re, new_im = re * sre - im * sim, re * sim + im * sre
-            if lag:
-                new_re, new_im = new_re + acc[:B, cols], new_im + acc[B:, cols]
-            if lag < LAGS:
-                acc[:B, cols] = new_re
-                acc[B:, cols] = new_im
-                return carry
-            hi, lo = split(jnp.concatenate([new_re, new_im], 0))
-            ihi, ilo = icat[:, : 2 * B], icat[:, 2 * B :]
-            result = (
-                jnp.dot(ihi, hi, preferred_element_type=jnp.float32)
-                + jnp.dot(ihi, lo, preferred_element_type=jnp.float32)
-                + jnp.dot(ilo, hi, preferred_element_type=jnp.float32)
-            )
-            out[:, cols] = (gate[:, cols].astype(jnp.float32) * result).astype(jnp.bfloat16)
-            return carry
-
-        lax.fori_loop(0, steps, convolve, 0)
-
+            acc_re = new_re if lag == 0 else acc_re + new_re
+            acc_im = new_im if lag == 0 else acc_im + new_im
+        hi, lo = split(jnp.concatenate([acc_re, acc_im], 0))
+        ihi, ilo = icat[:, : 2 * B], icat[:, 2 * B :]
+        result = (
+            jnp.dot(ihi, hi, preferred_element_type=jnp.float32)
+            + jnp.dot(ihi, lo, preferred_element_type=jnp.float32)
+            + jnp.dot(ilo, hi, preferred_element_type=jnp.float32)
+        )
+        out[:, cols] = (gate[:, cols].astype(jnp.float32) * result).astype(jnp.bfloat16)
+        leave(step).start()
+        return carry
+
+    wides = xv.shape[1] // WIDE
+    lax.fori_loop(0, wides, convolve, 0)
+
+    for step in range(wides):
+        leave(step).wait()
     each(xs, lambda copy: copy.wait_send())
     for k in spans:
         pl.when(has(k))(lambda copy=aways[k]: copy.wait_send())
@@ -352,7 +376,7 @@
         kernel,
         out_shape=jax.ShapeDtypeStruct((rows, channels), bf16),
         in_specs=[pl.BlockSpec(memory_space=pltpu.HBM)] * 7,
-        out_specs=pl.BlockSpec(memory_space=pltpu.VMEM),
+        out_specs=pl.BlockSpec(memory_space=pl.ANY),
         scratch_shapes=[
             pltpu.VMEM((rows, channels), bf16),
             pltpu.VMEM((rows, channels), bf16),
@@ -363,7 +387,8 @@
             pltpu.VMEM(icat.shape, bf16),
             pltpu.VMEM((LAGS, rows, channels), bf16),
             pltpu.VMEM((LAGS + 1, 2 * B, channels), f32),
-            pltpu.VMEM((2 * B, channels), f32),
+            pltpu.VMEM((LAGS + 1, 2 * B, 2 * B), bf16),
+            pltpu.VMEM((rows, channels), bf16),
             pltpu.VMEM((1, B), f32),
             pltpu.VMEM((3, 1, B), f32),
             pltpu.VMEM((1, B), f32),
@@ -381,6 +406,8 @@
             dma((LAGS + 1,)),
             dma((LAGS + 1,)),
             pltpu.SemaphoreType.REGULAR,
+            pltpu.SemaphoreType.REGULAR((LAGS,)),
+            dma((channels // WIDE,)),
         ],
         compiler_params=pltpu.CompilerParams(
             collective_id=0, has_side_effects=True, vmem_limit_bytes=60 * 1024 * 1024

time: 33.4 us -> 32 us (0.958)
  Pallas kernels: 31.6 us -> 30.1 us
    pallas_call x1, Pallas kernels: 31.6 us -> 30.1 us  [on_device(): pl.pallas_call(kernel, out_shape=jax.ShapeDtypeStruct((rows, channels), b...]
where the time goes in v3:
time: 32 us; the launch traced here: 31.8 us
  Pallas kernels  30.1 us (94%)
  local copies, waits for them, and re-layouts  1.67 us (5%)
    pallas_call x1, Pallas kernels, on_device(): pl.pallas_call(kernel, out_shape=jax.ShapeDtypeStruct((rows, channels), b...  30.1 us
    unnamed x1, local copies, waits for them, and re-layouts  1.67 us

profile of v3, /device:TPU:24, one launch (start us, length us, event | category | flops | bytes accessed | tf_op | source)
XLA Modules:
  0.0 31.8 jit_solution(18300493918032269277)
XLA Ops:
  0.0 30.1 %shard_map.73 = bf16[128,1024]{1,0:T(8,128)(2,1)} custom-call(bf16[128,1024]{1,0:T(8,128)(2,1)} %x_hbm.1, bf16[128,1024]{1,0:T(8,128)(2,1)} %gate_hbm.1, bf16[513,1024]{1,0:T(8,128)(2,1)} %taps_hbm.1, f32[1,1024]{1,0:T(1,128)} %bitcast.1, f32[256,128]{1,0:T(8,128)} %constant.6.clone.ftab_hbm, bf16[256,256]{1,0:T(8,128)(2,1)} %constant.7.clone.fcat_hbm, ...), custom_call_target="tpu_custom_call" | custom-call | tf_op jit(solution)/shard_map/pallas_call | solution.py:375
  30.1 1.7 %copy.9 = bf16[128,1024]{1,0:T(8,128)(2,1)} copy(bf16[128,1024]{1,0:T(8,128)(2,1)} %shard_map.73) | data formatting | bytes 524288

commit v4 on v3

--- a/solution.py
+++ b/solution.py
@@ -63,6 +63,7 @@
     xsum,
     near,
     away,
+    handed_sum,
     load_sem,
     own_send,
     fwd_send,
@@ -77,6 +78,8 @@
     ready,
     go,
     out_sem,
+    hub_send,
+    hub_recv,
 ):
     seq, chan = lax.axis_index("seq"), lax.axis_index("chan")
     count = lax.axis_size("seq")
@@ -95,6 +98,14 @@
 
     def beside(shift):
         return (seq, half * 4 + lax.rem(col + shift, 4))
+
+    row, side = lax.div(seq, 8), lax.rem(lax.div(seq, 2), 4) == 3
+    hub = jnp.logical_and(side, lax.rem(row, 2) == 1)
+    spoke = jnp.logical_and(side, lax.rem(row, 2) == 0)
+    lower = jnp.logical_not(upper)
+
+    def both(*conditions):
+        return functools.reduce(jnp.logical_and, conditions)
 
     def has(k):
         return jnp.logical_and(seq + k >= 0, seq + k < count)
@@ -119,15 +130,21 @@
 
     loads[0].start()
     barrier = pltpu.get_barrier_semaphore()
+    @pl.when(lower)
+    def _():
+        for k in range(-LAGS, LAGS + 1):
+            pl.when(has(k))(functools.partial(signal, barrier, across(k)))
+        pl.when(hub)(functools.partial(signal, barrier, across(-8)))
+
+        @pl.when(spoke)
+        def _():
+            signal(barrier, ahead(8))
+            pl.when(odd)(functools.partial(signal, barrier, ahead(7)))
+
     for shift in (1, 2, 3):
         signal(barrier, beside(shift))
     for k in lags:
         pl.when(has(k))(functools.partial(signal, barrier, ahead(k)))
-
-    @pl.when(jnp.logical_not(upper))
-    def _():
-        for k in range(-LAGS, LAGS + 1):
-            pl.when(has(k))(functools.partial(signal, barrier, across(k)))
 
     for load in loads[1:]:
         load.start()
@@ -142,7 +159,14 @@
     part[...] = jnp.sum(jnp.where(diagonal, gram, 0.0), axis=0, keepdims=True)
 
     before, after = jnp.minimum(seq, LAGS), jnp.minimum(count - 1 - seq, LAGS)
-    pl.semaphore_wait(barrier, 3 + before + half * (before + after + 1))
+    far = half * (before + after + 1 + spoke.astype(jnp.int32))
+    extra = (1 - half) * hub.astype(jnp.int32) * (2 - lax.rem(seq, 2))
+    pl.semaphore_wait(barrier, 3 + before + far + extra)
+
+    @pl.when(upper)
+    def _():
+        for k in spans:
+            pl.when(has(-k))(functools.partial(signal, ready, across(-k)))
 
     def remote(src, dst, send, recv, device):
         return pltpu.make_async_remote_copy(
@@ -191,11 +215,6 @@
 
     for k in (2, 1, 3, 4):
         pl.when(has(-k))(functools.partial(signal, go.at[k - 1], ahead(-k)))
-
-    @pl.when(upper)
-    def _():
-        for k in spans:
-            pl.when(has(-k))(functools.partial(signal, ready, across(-k)))
 
     for k in lags:
 
@@ -258,9 +277,22 @@
         remote(xsum, away.at[k], away_send.at[k], away_recv.at[k], across(k)) for k in spans
     ]
 
+    def direct(k):
+        if k > 1:
+            return has(k)
+        handed = both(upper, spoke) if k == 0 else both(upper, spoke, even)
+        return both(has(k), jnp.logical_not(handed))
+
+    to_hub = remote(xsum, handed_sum, hub_send.at[0], hub_recv, across(8))
+    from_hub = [
+        remote(handed_sum, away.at[k], hub_send.at[k + 1], away_recv.at[k], ahead(k - 8))
+        for k in (0, 1)
+    ]
+
     def send_away():
+        pl.when(both(upper, spoke))(lambda: to_hub.start())
         for k in spans:
-            pl.when(has(k))(lambda copy=aways[k]: copy.start())
+            pl.when(direct(k))(lambda copy=aways[k]: copy.start())
 
     pl.when(upper)(send_away)
     for k in lags:
@@ -283,6 +315,12 @@
     def _():
         pl.semaphore_wait(ready, after + 1)
         send_away()
+
+        @pl.when(hub)
+        def _():
+            to_hub.wait_recv()
+            from_hub[0].start()
+            pl.when(even)(lambda: from_hub[1].start())
 
     @pl.when(has(-4))
     def _():
@@ -352,7 +390,10 @@
         leave(step).wait()
     each(xs, lambda copy: copy.wait_send())
     for k in spans:
-        pl.when(has(k))(lambda copy=aways[k]: copy.wait_send())
+        pl.when(direct(k))(lambda copy=aways[k]: copy.wait_send())
+    pl.when(both(upper, spoke))(lambda: to_hub.wait_send())
+    pl.when(both(lower, hub))(lambda: from_hub[0].wait_send())
+    pl.when(both(lower, hub, even))(lambda: from_hub[1].wait_send())
     for k in lags:
         pl.when(has(k))(lambda copy=nears[k - 1]: copy.wait_send())
 
@@ -394,6 +435,7 @@
             pltpu.VMEM((1, B), f32),
             pltpu.VMEM((LAGS, 1, B), f32),
             pltpu.VMEM((LAGS + 1, 1, B), f32),
+            pltpu.VMEM((1, B), f32),
             dma((7,)),
             dma((CHUNKS,)),
             dma((CHUNKS,)),
@@ -408,6 +450,8 @@
             pltpu.SemaphoreType.REGULAR,
             pltpu.SemaphoreType.REGULAR((LAGS,)),
             dma((channels // WIDE,)),
+            dma((3,)),
+            dma,
         ],
         compiler_params=pltpu.CompilerParams(
             collective_id=0, has_side_effects=True, vmem_limit_bytes=60 * 1024 * 1024

time: 32 us -> 29.8 us (0.931)
  Pallas kernels: 30.1 us -> 27.9 us
    pallas_call x1, Pallas kernels: 30.1 us -> 27.9 us  [on_device(): pl.pallas_call(kernel, out_shape=jax.ShapeDtypeStruct((rows, channels), b...]
where the time goes in v4:
time: 29.8 us; the launch traced here: 29.6 us
  Pallas kernels  27.9 us (94%)
  local copies, waits for them, and re-layouts  1.67 us (6%)
    pallas_call x1, Pallas kernels, on_device(): pl.pallas_call(kernel, out_shape=jax.ShapeDtypeStruct((rows, channels), b...  27.9 us
    unnamed x1, local copies, waits for them, and re-layouts  1.67 us

profile of v4, /device:TPU:24, one launch (start us, length us, event | category | flops | bytes accessed | tf_op | source)
XLA Modules:
  0.0 29.6 jit_solution(16283968303124877380)
XLA Ops:
  0.0 27.9 %shard_map.73 = bf16[128,1024]{1,0:T(8,128)(2,1)} custom-call(bf16[128,1024]{1,0:T(8,128)(2,1)} %x_hbm.1, bf16[128,1024]{1,0:T(8,128)(2,1)} %gate_hbm.1, bf16[513,1024]{1,0:T(8,128)(2,1)} %taps_hbm.1, f32[1,1024]{1,0:T(1,128)} %bitcast.1, f32[256,128]{1,0:T(8,128)} %constant.6.clone.ftab_hbm, bf16[256,256]{1,0:T(8,128)(2,1)} %constant.7.clone.fcat_hbm, ...), custom_call_target="tpu_custom_call" | custom-call | tf_op jit(solution)/shard_map/pallas_call | solution.py:416
  27.9 1.7 %copy.9 = bf16[128,1024]{1,0:T(8,128)(2,1)} copy(bf16[128,1024]{1,0:T(8,128)(2,1)} %shard_map.73) | data formatting | bytes 524288

commit v5 on v4

--- a/solution.py
+++ b/solution.py
@@ -14,7 +14,7 @@
 LAGS = 4
 CW = 256
 WIDE = 512
-CHUNKS = 4
+CHUNKS = 2
 ROWS = B // CHUNKS
 
 
@@ -32,10 +32,9 @@
     def halves(table):
         table = table.astype(np.float32)
         hi = table.astype(jnp.bfloat16)
-        lo = (table - hi.astype(np.float32)).astype(jnp.bfloat16)
-        return np.concatenate([hi, lo], 1)
-
-    return forward.astype(np.float32), halves(forward), halves(inverse)
+        return [hi, (table - hi.astype(np.float32)).astype(jnp.bfloat16)]
+
+    return np.concatenate([np.concatenate(halves(forward), 1)] + halves(inverse), 0)
 
 
 def kernel(
@@ -43,17 +42,13 @@
     gate_hbm,
     taps_hbm,
     skip_hbm,
-    ftab_hbm,
-    fcat_hbm,
-    icat_hbm,
+    tab_hbm,
     out_hbm,
     xv,
     gate,
     taps,
     skip,
-    ftab,
-    fcat,
-    icat,
+    tab,
     halo,
     spec,
     fs,
@@ -65,21 +60,16 @@
     away,
     handed_sum,
     load_sem,
-    own_send,
-    fwd_send,
+    next_send,
     mate_send,
-    halo_recv,
-    x_send,
-    x_recv,
-    near_send,
-    near_recv,
-    away_send,
-    away_recv,
-    ready,
-    go,
+    next_recv,
+    mate_recv,
+    x_sem,
+    near_sem,
+    away_sem,
+    hub_sem,
+    greet,
     out_sem,
-    hub_send,
-    hub_recv,
 ):
     seq, chan = lax.axis_index("seq"), lax.axis_index("chan")
     count = lax.axis_size("seq")
@@ -118,11 +108,9 @@
         for n, (src, dst) in enumerate(
             [
                 (x_hbm, xv),
-                (fcat_hbm, fcat),
+                (tab_hbm, tab),
                 (taps_hbm, taps),
                 (skip_hbm, skip),
-                (ftab_hbm, ftab),
-                (icat_hbm, icat),
                 (gate_hbm, gate),
             ]
         )
@@ -166,7 +154,7 @@
     @pl.when(upper)
     def _():
         for k in spans:
-            pl.when(has(-k))(functools.partial(signal, ready, across(-k)))
+            pl.when(has(-k))(functools.partial(signal, greet.at[2], across(-k)))
 
     def remote(src, dst, send, recv, device):
         return pltpu.make_async_remote_copy(
@@ -181,46 +169,64 @@
     def piece(n):
         return pl.ds(n * ROWS, ROWS)
 
-    def to_next(src, slot, n, send):
+    def to_next(src, slot, n, rows):
         return remote(
-            src.at[piece(n)], halo.at[slot, piece(n)], send.at[n], halo_recv.at[slot, n], ahead(2)
+            src.at[rows],
+            halo.at[slot, rows],
+            next_send.at[slot // 2],
+            next_recv.at[slot // 2, n],
+            ahead(2),
         )
 
-    def to_mate(src, slot, n):
+    def to_mate(src, slot, rows):
         return remote(
-            src.at[piece(n)],
-            halo.at[slot, piece(n)],
-            mate_send.at[slot // 2, n],
-            halo_recv.at[slot, n],
+            src.at[rows],
+            halo.at[slot, rows],
+            mate_send.at[slot // 2],
+            mate_recv.at[slot // 2],
             ahead(1 - 2 * lax.rem(seq, 2)),
         )
 
     pieces = range(CHUNKS)
-    own = [to_next(x_hbm, 1, n, own_send) for n in pieces]
-    onward = [to_next(halo.at[1], 3, n, fwd_send) for n in pieces]
-    even_first = [to_mate(x_hbm, 0, n) for n in pieces]
-    even_second = [to_mate(halo.at[1], 2, n) for n in pieces]
-    odd_first = [to_mate(halo.at[1], 0, n) for n in pieces]
-    odd_second = [to_mate(halo.at[3], 2, n) for n in pieces]
+    whole = pl.ds(0, B)
+    own = [to_next(x_hbm, 1, n, piece(n)) for n in pieces]
+    onward = [to_next(halo.at[1], 3, n, piece(n)) for n in pieces]
+    even_first = to_mate(x_hbm, 0, whole)
+    even_second = [to_mate(halo.at[1], 2, piece(n)) for n in pieces]
+    odd_first = [to_mate(halo.at[1], 0, piece(n)) for n in pieces]
+    odd_second = [to_mate(halo.at[3], 2, piece(n)) for n in pieces]
+    all_next = [to_next(halo.at[slot], slot, 0, whole) for slot in (1, 3)]
+    all_mate = [to_mate(halo.at[slot], slot, whole) for slot in (0, 2)]
+
+    def gather(ref, sems, amount, most):
+        def on(act):
+            for n in range(1, most + 1):
+                rows = ref.at[pl.ds(0, n)]
+                copy = remote(rows, rows, sems.at[0], sems.at[1], beside(1))
+                pl.when(amount == n)(functools.partial(act, copy))
+
+        return on
 
     def each(copies, act):
         for copy in copies:
             act(copy)
 
     xs = [
-        remote(part, xpart.at[d - 1], x_send.at[d - 1], x_recv.at[d - 1], beside(d))
+        remote(part, xpart.at[d - 1], x_sem.at[0], x_sem.at[1], beside(d))
         for d in (1, 2, 3)
     ]
     each(xs, lambda copy: copy.start())
 
     for k in (2, 1, 3, 4):
-        pl.when(has(-k))(functools.partial(signal, go.at[k - 1], ahead(-k)))
+        pl.when(has(-k))(functools.partial(signal, greet.at[(k - 1) // 2], ahead(-k)))
 
     for k in lags:
 
         @pl.when(seq < k)
         def _():
             halo[k - 1] = jnp.zeros(halo.shape[1:], halo.dtype)
+
+    every_x = remote(xpart, xpart, x_sem.at[0], x_sem.at[1], beside(1))
 
     each(loads[1:4], lambda copy: copy.wait())
 
@@ -231,7 +237,7 @@
             if lag < LAGS:
                 block = taps[lag * B : (lag + 1) * B, cols]
                 here = jnp.dot(
-                    fcat[...],
+                    tab[: 2 * B],
                     jnp.concatenate([block, block], 0),
                     preferred_element_type=jnp.float32,
                 )
@@ -254,27 +260,17 @@
     steps = xv.shape[1] // CW
     lax.fori_loop(0, steps, filter_spectra, 0)
 
-    @pl.when(has(2))
-    def _():
-        pl.semaphore_wait(go.at[1], 1)
-        each(own, lambda copy: copy.start())
-
-    @pl.when(has(1))
-    def _():
-        pl.semaphore_wait(go.at[0], 1)
-
-        @pl.when(even)
-        def _():
-            each(even_first, lambda copy: copy.start())
-
-    each(xs, lambda copy: copy.wait_recv())
+    pl.when(has(1))(lambda: pl.semaphore_wait(greet.at[0], jnp.minimum(after, 2)))
+    pl.when(has(2))(lambda: each(own, lambda copy: copy.start()))
+    pl.when(even)(lambda: even_first.start())
+    every_x.wait_recv()
     xsum[...] = part[...] + xpart[0] + xpart[1] + xpart[2]
     nears = [
-        remote(xsum, near.at[k - 1], near_send.at[k - 1], near_recv.at[k - 1], ahead(k))
+        remote(xsum, near.at[k - 1], near_sem.at[0], near_sem.at[1], ahead(k))
         for k in lags
     ]
     aways = [
-        remote(xsum, away.at[k], away_send.at[k], away_recv.at[k], across(k)) for k in spans
+        remote(xsum, away.at[k], away_sem.at[0], away_sem.at[1], across(k)) for k in spans
     ]
 
     def direct(k):
@@ -283,9 +279,9 @@
         handed = both(upper, spoke) if k == 0 else both(upper, spoke, even)
         return both(has(k), jnp.logical_not(handed))
 
-    to_hub = remote(xsum, handed_sum, hub_send.at[0], hub_recv, across(8))
+    to_hub = remote(xsum, handed_sum.at[0], away_sem.at[0], hub_sem.at[1], across(8))
     from_hub = [
-        remote(handed_sum, away.at[k], hub_send.at[k + 1], away_recv.at[k], ahead(k - 8))
+        remote(handed_sum.at[0], away.at[k], hub_sem.at[0], away_sem.at[1], ahead(k - 8))
         for k in (0, 1)
     ]
 
@@ -295,13 +291,9 @@
             pl.when(direct(k))(lambda copy=aways[k]: copy.start())
 
     pl.when(upper)(send_away)
+    pl.when(has(3))(lambda: pl.semaphore_wait(greet.at[1], after - 2))
     for k in lags:
-
-        @pl.when(has(k))
-        def _():
-            if k > 2:
-                pl.semaphore_wait(go.at[k - 1], 1)
-            nears[k - 1].start()
+        pl.when(has(k))(lambda copy=nears[k - 1]: copy.start())
 
     @pl.when(has(-2))
     def _():
@@ -313,7 +305,7 @@
 
     @pl.when(jnp.logical_not(upper))
     def _():
-        pl.semaphore_wait(ready, after + 1)
+        pl.semaphore_wait(greet.at[2], after + 1)
         send_away()
 
         @pl.when(hub)
@@ -338,25 +330,28 @@
         scale = lax.rsqrt(sums * (1.0 / D) + 1e-06)
         if lag:
             scale = jnp.where(seq >= lag, scale, 0.0)
-        hi, lo = split(ftab[...] * scale)
+        hi, lo = split((tab[: 2 * B, :B].astype(jnp.float32) + tab[: 2 * B, B:].astype(jnp.float32)) * scale)
         fs[lag, :, :B] = hi
         fs[lag, :, B:] = lo
 
-    def arrived(lag):
-        if lag in (1, 3):
-            each(odd_first if lag == 1 else odd_second, lambda copy: copy.wait_recv())
-        nears[lag - 1].wait_recv()
-        aways[lag].wait_recv()
-
     def leave(step):
         cols = pl.ds(pl.multiple_of(step * WIDE, WIDE), WIDE)
-        return pltpu.make_async_copy(out.at[:, cols], out_hbm.at[:, cols], out_sem.at[step])
-
+        return pltpu.make_async_copy(out.at[:, cols], out_hbm.at[:, cols], out_sem)
+
+    def sent(*copies):
+        each(copies, lambda copy: copy.wait_send())
+
+    every_x.wait_send()
+    gather(near, near_sem, after, LAGS)(lambda copy: copy.wait_send())
+    pl.when(has(2))(lambda: sent(all_next[0]))
+    pl.when(both(has(2), has(-2)))(lambda: sent(all_next[1]))
+    pl.when(jnp.logical_or(even, has(-2)))(lambda: sent(all_mate[0]))
+    pl.when(jnp.logical_or(both(even, has(-2)), has(-4)))(lambda: sent(all_mate[1]))
+    pl.when(has(-1))(lambda: all_mate[0].wait_recv())
+    pl.when(has(-3))(lambda: all_mate[1].wait_recv())
+    gather(near, near_sem, before, LAGS)(lambda copy: copy.wait_recv())
+    gather(away, away_sem, before + 1, LAGS + 1)(lambda copy: copy.wait_recv())
     for lag in spans:
-        if lag == 0:
-            aways[0].wait_recv()
-        else:
-            pl.when(seq >= lag)(functools.partial(arrived, lag))
         scaled(lag)
 
     def convolve(step, carry):
@@ -373,7 +368,7 @@
             acc_re = new_re if lag == 0 else acc_re + new_re
             acc_im = new_im if lag == 0 else acc_im + new_im
         hi, lo = split(jnp.concatenate([acc_re, acc_im], 0))
-        ihi, ilo = icat[:, : 2 * B], icat[:, 2 * B :]
+        ihi, ilo = tab[2 * B : 3 * B], tab[3 * B :]
         result = (
             jnp.dot(ihi, hi, preferred_element_type=jnp.float32)
             + jnp.dot(ihi, lo, preferred_element_type=jnp.float32)
@@ -386,46 +381,29 @@
     wides = xv.shape[1] // WIDE
     lax.fori_loop(0, wides, convolve, 0)
 
-    for step in range(wides):
-        leave(step).wait()
-    each(xs, lambda copy: copy.wait_send())
-    for k in spans:
-        pl.when(direct(k))(lambda copy=aways[k]: copy.wait_send())
-    pl.when(both(upper, spoke))(lambda: to_hub.wait_send())
-    pl.when(both(lower, hub))(lambda: from_hub[0].wait_send())
-    pl.when(both(lower, hub, even))(lambda: from_hub[1].wait_send())
-    for k in lags:
-        pl.when(has(k))(lambda copy=nears[k - 1]: copy.wait_send())
-
-    def sent(copies):
-        each(copies, lambda copy: copy.wait_send())
-
-    pl.when(has(2))(lambda: sent(own))
-    pl.when(jnp.logical_and(has(2), has(-2)))(lambda: sent(onward))
-    pl.when(even)(lambda: sent(even_first))
-    pl.when(jnp.logical_and(even, has(-2)))(lambda: sent(even_second))
-    pl.when(jnp.logical_and(odd, has(-2)))(lambda: sent(odd_first))
-    pl.when(jnp.logical_and(odd, has(-4)))(lambda: sent(odd_second))
+    left = after + 1 - both(upper, spoke, even).astype(jnp.int32)
+    gather(away, away_sem, left, LAGS + 1)(lambda copy: copy.wait_send())
+    handed_on = both(lower, hub).astype(jnp.int32) * (2 - lax.rem(seq, 2))
+    gather(handed_sum, hub_sem, handed_on, 2)(lambda copy: copy.wait_send())
+    pltpu.make_async_copy(out, out_hbm, out_sem).wait()
 
 
 def on_device(inputs, gating, long_filter, skip_scale):
     rows, channels = inputs.shape
     bf16, f32 = jnp.bfloat16, jnp.float32
-    ftab, fcat, icat = tables()
+    tab = tables()
     dma = pltpu.SemaphoreType.DMA
     return pl.pallas_call(
         kernel,
         out_shape=jax.ShapeDtypeStruct((rows, channels), bf16),
-        in_specs=[pl.BlockSpec(memory_space=pltpu.HBM)] * 7,
+        in_specs=[pl.BlockSpec(memory_space=pltpu.HBM)] * 5,
         out_specs=pl.BlockSpec(memory_space=pl.ANY),
         scratch_shapes=[
             pltpu.VMEM((rows, channels), bf16),
             pltpu.VMEM((rows, channels), bf16),
             pltpu.VMEM(long_filter.shape, bf16),
             pltpu.VMEM((1, channels), f32),
-            pltpu.VMEM(ftab.shape, f32),
-            pltpu.VMEM(fcat.shape, bf16),
-            pltpu.VMEM(icat.shape, bf16),
+            pltpu.VMEM(tab.shape, bf16),
             pltpu.VMEM((LAGS, rows, channels), bf16),
             pltpu.VMEM((LAGS + 1, 2 * B, channels), f32),
             pltpu.VMEM((LAGS + 1, 2 * B, 2 * B), bf16),
@@ -435,28 +413,23 @@
             pltpu.VMEM((1, B), f32),
             pltpu.VMEM((LAGS, 1, B), f32),
             pltpu.VMEM((LAGS + 1, 1, B), f32),
-            pltpu.VMEM((1, B), f32),
-            dma((7,)),
-            dma((CHUNKS,)),
-            dma((CHUNKS,)),
+            pltpu.VMEM((2, 1, B), f32),
+            dma((5,)),
+            dma((2,)),
+            dma((2,)),
             dma((2, CHUNKS)),
-            dma((LAGS, CHUNKS)),
-            dma((3,)),
-            dma((3,)),
-            dma((LAGS,)),
-            dma((LAGS,)),
-            dma((LAGS + 1,)),
-            dma((LAGS + 1,)),
-            pltpu.SemaphoreType.REGULAR,
-            pltpu.SemaphoreType.REGULAR((LAGS,)),
-            dma((channels // WIDE,)),
-            dma((3,)),
+            dma((2,)),
+            dma((2,)),
+            dma((2,)),
+            dma((2,)),
+            dma((2,)),
+            pltpu.SemaphoreType.REGULAR((3,)),
             dma,
         ],
         compiler_params=pltpu.CompilerParams(
             collective_id=0, has_side_effects=True, vmem_limit_bytes=60 * 1024 * 1024
         ),
-    )(inputs, gating, long_filter, skip_scale[None, :], ftab, fcat, icat)
+    )(inputs, gating, long_filter, skip_scale[None, :], tab)
 
 
 def solution(mesh):

time: 29.8 us -> 30.2 us (1.013)
  the two profiles are of different devices: /device:TPU:24 before, /device:TPU:487 now
where the time goes in v5:
time: 30.2 us; the launch traced here: 30.1 us
  Pallas kernels  28.4 us (94%)
  local copies, waits for them, and re-layouts  1.67 us (6%)
    pallas_call x1, Pallas kernels, on_device(): pl.pallas_call(kernel, out_shape=jax.ShapeDtypeStruct((rows, channels), b...  28.4 us
    unnamed x1, local copies, waits for them, and re-layouts  1.67 us

profile of v5, /device:TPU:487, one launch (start us, length us, event | category | flops | bytes accessed | tf_op | source)
XLA Modules:
  0.0 30.1 jit_solution(9900389964095731864)
XLA Ops:
  0.0 28.4 %shard_map.55 = bf16[128,1024]{1,0:T(8,128)(2,1)} custom-call(bf16[128,1024]{1,0:T(8,128)(2,1)} %x_hbm.1, bf16[128,1024]{1,0:T(8,128)(2,1)} %gate_hbm.1, bf16[513,1024]{1,0:T(8,128)(2,1)} %taps_hbm.1, f32[1,1024]{1,0:T(1,128)} %bitcast.1, bf16[512,256]{1,0:T(8,128)(2,1)} %constant.2.clone.tab_hbm), custom_call_target="tpu_custom_call" | custom-call | tf_op jit(solution)/shard_map/pallas_call | solution.py:396
  28.4 1.7 %copy.7 = bf16[128,1024]{1,0:T(8,128)(2,1)} copy(bf16[128,1024]{1,0:T(8,128)(2,1)} %shard_map.55) | data formatting | bytes 524288

commit v6 on v5

--- a/solution.py
+++ b/solution.py
@@ -14,7 +14,7 @@
 LAGS = 4
 CW = 256
 WIDE = 512
-CHUNKS = 2
+CHUNKS = 4
 ROWS = B // CHUNKS
 
 
@@ -146,89 +146,14 @@
     )
     part[...] = jnp.sum(jnp.where(diagonal, gram, 0.0), axis=0, keepdims=True)
 
-    before, after = jnp.minimum(seq, LAGS), jnp.minimum(count - 1 - seq, LAGS)
-    far = half * (before + after + 1 + spoke.astype(jnp.int32))
-    extra = (1 - half) * hub.astype(jnp.int32) * (2 - lax.rem(seq, 2))
-    pl.semaphore_wait(barrier, 3 + before + far + extra)
-
-    @pl.when(upper)
-    def _():
-        for k in spans:
-            pl.when(has(-k))(functools.partial(signal, greet.at[2], across(-k)))
-
-    def remote(src, dst, send, recv, device):
-        return pltpu.make_async_remote_copy(
-            src_ref=src,
-            dst_ref=dst,
-            send_sem=send,
-            recv_sem=recv,
-            device_id=device,
-            device_id_type=MESH,
-        )
-
-    def piece(n):
-        return pl.ds(n * ROWS, ROWS)
-
-    def to_next(src, slot, n, rows):
-        return remote(
-            src.at[rows],
-            halo.at[slot, rows],
-            next_send.at[slot // 2],
-            next_recv.at[slot // 2, n],
-            ahead(2),
-        )
-
-    def to_mate(src, slot, rows):
-        return remote(
-            src.at[rows],
-            halo.at[slot, rows],
-            mate_send.at[slot // 2],
-            mate_recv.at[slot // 2],
-            ahead(1 - 2 * lax.rem(seq, 2)),
-        )
-
-    pieces = range(CHUNKS)
-    whole = pl.ds(0, B)
-    own = [to_next(x_hbm, 1, n, piece(n)) for n in pieces]
-    onward = [to_next(halo.at[1], 3, n, piece(n)) for n in pieces]
-    even_first = to_mate(x_hbm, 0, whole)
-    even_second = [to_mate(halo.at[1], 2, piece(n)) for n in pieces]
-    odd_first = [to_mate(halo.at[1], 0, piece(n)) for n in pieces]
-    odd_second = [to_mate(halo.at[3], 2, piece(n)) for n in pieces]
-    all_next = [to_next(halo.at[slot], slot, 0, whole) for slot in (1, 3)]
-    all_mate = [to_mate(halo.at[slot], slot, whole) for slot in (0, 2)]
-
-    def gather(ref, sems, amount, most):
-        def on(act):
-            for n in range(1, most + 1):
-                rows = ref.at[pl.ds(0, n)]
-                copy = remote(rows, rows, sems.at[0], sems.at[1], beside(1))
-                pl.when(amount == n)(functools.partial(act, copy))
-
-        return on
-
-    def each(copies, act):
-        for copy in copies:
-            act(copy)
-
-    xs = [
-        remote(part, xpart.at[d - 1], x_sem.at[0], x_sem.at[1], beside(d))
-        for d in (1, 2, 3)
-    ]
-    each(xs, lambda copy: copy.start())
-
-    for k in (2, 1, 3, 4):
-        pl.when(has(-k))(functools.partial(signal, greet.at[(k - 1) // 2], ahead(-k)))
-
     for k in lags:
 
         @pl.when(seq < k)
         def _():
             halo[k - 1] = jnp.zeros(halo.shape[1:], halo.dtype)
 
-    every_x = remote(xpart, xpart, x_sem.at[0], x_sem.at[1], beside(1))
-
-    each(loads[1:4], lambda copy: copy.wait())
+    for load in loads[1:4]:
+        load.wait()
 
     def filter_spectra(step, carry):
         cols = pl.ds(pl.multiple_of(step * CW, CW), CW)
@@ -259,6 +184,82 @@
 
     steps = xv.shape[1] // CW
     lax.fori_loop(0, steps, filter_spectra, 0)
+
+    before, after = jnp.minimum(seq, LAGS), jnp.minimum(count - 1 - seq, LAGS)
+    far = half * (before + after + 1 + spoke.astype(jnp.int32))
+    extra = (1 - half) * hub.astype(jnp.int32) * (2 - lax.rem(seq, 2))
+    pl.semaphore_wait(barrier, 3 + before + far + extra)
+
+    @pl.when(upper)
+    def _():
+        for k in spans:
+            pl.when(has(-k))(functools.partial(signal, greet.at[2], across(-k)))
+
+    def remote(src, dst, send, recv, device):
+        return pltpu.make_async_remote_copy(
+            src_ref=src,
+            dst_ref=dst,
+            send_sem=send,
+            recv_sem=recv,
+            device_id=device,
+            device_id_type=MESH,
+        )
+
+    def piece(n):
+        return pl.ds(n * ROWS, ROWS)
+
+    def to_next(src, slot, n, rows):
+        return remote(
+            src.at[rows],
+            halo.at[slot, rows],
+            next_send.at[slot // 2],
+            next_recv.at[slot // 2, n],
+            ahead(2),
+        )
+
+    def to_mate(src, slot, rows):
+        return remote(
+            src.at[rows],
+            halo.at[slot, rows],
+            mate_send.at[slot // 2],
+            mate_recv.at[slot // 2],
+            ahead(1 - 2 * lax.rem(seq, 2)),
+        )
+
+    pieces = range(CHUNKS)
+    whole = pl.ds(0, B)
+    own = [to_next(x_hbm, 1, n, piece(n)) for n in pieces]
+    onward = [to_next(halo.at[1], 3, n, piece(n)) for n in pieces]
+    even_first = to_mate(x_hbm, 0, whole)
+    even_second = [to_mate(halo.at[1], 2, piece(n)) for n in pieces]
+    odd_first = [to_mate(halo.at[1], 0, piece(n)) for n in pieces]
+    odd_second = [to_mate(halo.at[3], 2, piece(n)) for n in pieces]
+    all_next = [to_next(halo.at[slot], slot, 0, whole) for slot in (1, 3)]
+    all_mate = [to_mate(halo.at[slot], slot, whole) for slot in (0, 2)]
+
+    def gather(ref, sems, amount, most):
+        def on(act):
+            for n in range(1, most + 1):
+                rows = ref.at[pl.ds(0, n)]
+                copy = remote(rows, rows, sems.at[0], sems.at[1], beside(1))
+                pl.when(amount == n)(functools.partial(act, copy))
+
+        return on
+
+    def each(copies, act):
+        for copy in copies:
+            act(copy)
+
+    xs = [
+        remote(part, xpart.at[d - 1], x_sem.at[0], x_sem.at[1], beside(d))
+        for d in (1, 2, 3)
+    ]
+    each(xs, lambda copy: copy.start())
+
+    for k in (2, 1, 3, 4):
+        pl.when(has(-k))(functools.partial(signal, greet.at[(k - 1) // 2], ahead(-k)))
+
+    every_x = remote(xpart, xpart, x_sem.at[0], x_sem.at[1], beside(1))
 
     pl.when(has(1))(lambda: pl.semaphore_wait(greet.at[0], jnp.minimum(after, 2)))
     pl.when(has(2))(lambda: each(own, lambda copy: copy.start()))

time: 30.2 us -> 30.7 us (1.017)
  the two profiles are of different devices: /device:TPU:487 before, /device:TPU:24 now
where the time goes in v6:
time: 30.7 us; the launch traced here: 30.5 us
  Pallas kernels  28.8 us (94%)
  local copies, waits for them, and re-layouts  1.67 us (5%)
    pallas_call x1, Pallas kernels, on_device(): pl.pallas_call(kernel, out_shape=jax.ShapeDtypeStruct((rows, channels), b...  28.8 us
    unnamed x1, local copies, waits for them, and re-layouts  1.67 us

profile of v6, /device:TPU:24, one launch (start us, length us, event | category | flops | bytes accessed | tf_op | source)
XLA Modules:
  0.0 30.5 jit_solution(4301874477299402251)
XLA Ops:
  0.0 28.8 %shard_map.55 = bf16[128,1024]{1,0:T(8,128)(2,1)} custom-call(bf16[128,1024]{1,0:T(8,128)(2,1)} %x_hbm.1, bf16[128,1024]{1,0:T(8,128)(2,1)} %gate_hbm.1, bf16[513,1024]{1,0:T(8,128)(2,1)} %taps_hbm.1, f32[1,1024]{1,0:T(1,128)} %bitcast.1, bf16[512,256]{1,0:T(8,128)(2,1)} %constant.2.clone.tab_hbm), custom_call_target="tpu_custom_call" | custom-call | tf_op jit(solution)/shard_map/pallas_call | solution.py:397
  28.9 1.7 %copy.7 = bf16[128,1024]{1,0:T(8,128)(2,1)} copy(bf16[128,1024]{1,0:T(8,128)(2,1)} %shard_map.55) | data formatting | bytes 524288

commit v7 on v5

--- a/solution.py
+++ b/solution.py
@@ -14,7 +14,7 @@
 LAGS = 4
 CW = 256
 WIDE = 512
-CHUNKS = 2
+CHUNKS = 4
 ROWS = B // CHUNKS
 
 
@@ -220,6 +220,10 @@
     for k in (2, 1, 3, 4):
         pl.when(has(-k))(functools.partial(signal, greet.at[(k - 1) // 2], ahead(-k)))
 
+    pl.when(has(1))(lambda: pl.semaphore_wait(greet.at[0], jnp.minimum(after, 2)))
+    pl.when(has(2))(lambda: each(own, lambda copy: copy.start()))
+    pl.when(even)(lambda: even_first.start())
+
     for k in lags:
 
         @pl.when(seq < k)
@@ -260,9 +264,6 @@
     steps = xv.shape[1] // CW
     lax.fori_loop(0, steps, filter_spectra, 0)
 
-    pl.when(has(1))(lambda: pl.semaphore_wait(greet.at[0], jnp.minimum(after, 2)))
-    pl.when(has(2))(lambda: each(own, lambda copy: copy.start()))
-    pl.when(even)(lambda: even_first.start())
     every_x.wait_recv()
     xsum[...] = part[...] + xpart[0] + xpart[1] + xpart[2]
     nears = [
@@ -343,10 +344,6 @@
 
     every_x.wait_send()
     gather(near, near_sem, after, LAGS)(lambda copy: copy.wait_send())
-    pl.when(has(2))(lambda: sent(all_next[0]))
-    pl.when(both(has(2), has(-2)))(lambda: sent(all_next[1]))
-    pl.when(jnp.logical_or(even, has(-2)))(lambda: sent(all_mate[0]))
-    pl.when(jnp.logical_or(both(even, has(-2)), has(-4)))(lambda: sent(all_mate[1]))
     pl.when(has(-1))(lambda: all_mate[0].wait_recv())
     pl.when(has(-3))(lambda: all_mate[1].wait_recv())
     gather(near, near_sem, before, LAGS)(lambda copy: copy.wait_recv())
@@ -381,6 +378,10 @@
     wides = xv.shape[1] // WIDE
     lax.fori_loop(0, wides, convolve, 0)
 
+    pl.when(has(2))(lambda: sent(all_next[0]))
+    pl.when(both(has(2), has(-2)))(lambda: sent(all_next[1]))
+    pl.when(jnp.logical_or(even, has(-2)))(lambda: sent(all_mate[0]))
+    pl.when(jnp.logical_or(both(even, has(-2)), has(-4)))(lambda: sent(all_mate[1]))
     left = after + 1 - both(upper, spoke, even).astype(jnp.int32)
     gather(away, away_sem, left, LAGS + 1)(lambda copy: copy.wait_send())
     handed_on = both(lower, hub).astype(jnp.int32) * (2 - lax.rem(seq, 2))

time: 30.2 us -> 29.8 us (0.987)
  the two profiles are of different devices: /device:TPU:487 before, /device:TPU:486 now
where the time goes in v7:
time: 29.8 us; the launch traced here: 29.7 us
  Pallas kernels  28 us (94%)
  local copies, waits for them, and re-layouts  1.67 us (6%)
    pallas_call x1, Pallas kernels, on_device(): pl.pallas_call(kernel, out_shape=jax.ShapeDtypeStruct((rows, channels), b...  28 us
    unnamed x1, local copies, waits for them, and re-layouts  1.67 us

profile of v7, /device:TPU:486, one launch (start us, length us, event | category | flops | bytes accessed | tf_op | source)
XLA Modules:
  0.0 29.7 jit_solution(8294592380048654921)
XLA Ops:
  0.0 28.0 %shard_map.55 = bf16[128,1024]{1,0:T(8,128)(2,1)} custom-call(bf16[128,1024]{1,0:T(8,128)(2,1)} %x_hbm.1, bf16[128,1024]{1,0:T(8,128)(2,1)} %gate_hbm.1, bf16[513,1024]{1,0:T(8,128)(2,1)} %taps_hbm.1, f32[1,1024]{1,0:T(1,128)} %bitcast.1, bf16[512,256]{1,0:T(8,128)(2,1)} %constant.2.clone.tab_hbm), custom_call_target="tpu_custom_call" | custom-call | tf_op jit(solution)/shard_map/pallas_call | solution.py:397
  28.0 1.7 %copy.7 = bf16[128,1024]{1,0:T(8,128)(2,1)} copy(bf16[128,1024]{1,0:T(8,128)(2,1)} %shard_map.55) | data formatting | bytes 524288

commit v8 on v7

--- a/solution.py
+++ b/solution.py
@@ -14,7 +14,7 @@
 LAGS = 4
 CW = 256
 WIDE = 512
-CHUNKS = 4
+CHUNKS = 8
 ROWS = B // CHUNKS
 
 

time: 29.8 us -> 29.9 us (level)
  the two profiles are of different devices: /device:TPU:486 before, /device:TPU:484 now
where the time goes in v8:
time: 29.9 us; the launch traced here: 29.7 us
  Pallas kernels  28 us (94%)
  local copies, waits for them, and re-layouts  1.67 us (6%)
    pallas_call x1, Pallas kernels, on_device(): pl.pallas_call(kernel, out_shape=jax.ShapeDtypeStruct((rows, channels), b...  28 us
    unnamed x1, local copies, waits for them, and re-layouts  1.67 us

profile of v8, /device:TPU:484, one launch (start us, length us, event | category | flops | bytes accessed | tf_op | source)
XLA Modules:
  0.0 29.7 jit_solution(10762730389681829674)
XLA Ops:
  0.0 28.0 %shard_map.55 = bf16[128,1024]{1,0:T(8,128)(2,1)} custom-call(bf16[128,1024]{1,0:T(8,128)(2,1)} %x_hbm.1, bf16[128,1024]{1,0:T(8,128)(2,1)} %gate_hbm.1, bf16[513,1024]{1,0:T(8,128)(2,1)} %taps_hbm.1, f32[1,1024]{1,0:T(1,128)} %bitcast.1, bf16[512,256]{1,0:T(8,128)(2,1)} %constant.2.clone.tab_hbm), custom_call_target="tpu_custom_call" | custom-call | tf_op jit(solution)/shard_map/pallas_call | solution.py:397
  28.0 1.7 %copy.7 = bf16[128,1024]{1,0:T(8,128)(2,1)} copy(bf16[128,1024]{1,0:T(8,128)(2,1)} %shard_map.55) | data formatting | bytes 524288
